TPU v7x, 128 devices: a whole 4x4x4 slice. The times are simulated.
128 devices in a mesh: fsdp: 8 (over z, x_hi), ctx: 8 (over y, core), tp: 2 (over x_lo).
Axes of the slice: x: 4 (x_hi: 2, x_lo: 2; x = x_hi * 2 + x_lo), y: 4, z: 4, core: 2. Of those that a mesh axis runs over, the one named last changes fastest.
Arguments:
- inputs: float32 [8, 1024, 1152], P('fsdp', 'ctx'), may hold values from -6 to 6
- positions: int32 [8, 1024], P('fsdp', 'ctx'), may hold values from 0 to 959, as said below
- norm_gains: bfloat16 [1152, 4], P('fsdp'), may hold values from 0.5 to 1.5
- head_gains: bfloat16 [2, 256], replicated, may hold values from 0.3984375 to 1.59375
- attn_split: bfloat16 [1152, 2, 1024], P('fsdp', None, 'tp'), may hold values from -0.1875 to 0.1875
- attn_shared: bfloat16 [1152, 2, 256], P('fsdp'), may hold values from -0.1875 to 0.1875
- ffn_gate_up: bfloat16 [1152, 2, 6912], P('fsdp', None, 'tp'), may hold values from -0.1875 to 0.1875
- ffn_down: bfloat16 [1152, 6912], P('fsdp', 'tp'), may hold values from -0.078125 to 0.078125
- cotangent: float32 [8, 1024, 1152], P('fsdp', 'ctx'), may hold values from -6 to 6
Outputs:
- output: float32 [8, 1024, 1152], P('fsdp', 'ctx')
- d_inputs: float32 [8, 1024, 1152], P('fsdp', 'ctx')
- d_norm_gains: float32 [1152, 4], P('fsdp')
- d_head_gains: float32 [2, 256], replicated
- d_attn_split: float32 [1152, 2, 1024], P('fsdp', None, 'tp')
- d_attn_shared: float32 [1152, 2, 256], P('fsdp')
- d_gate_up: float32 [1152, 2, 6912], P('fsdp', None, 'tp')
- d_down: float32 [1152, 6912], P('fsdp', 'tp')
Inputs may be any that keep to these rules, and one draw needn't show every extreme that they name: `positions`: each sequence is packed with documents of 64 to 960 tokens, the last one possibly cut by the sequence's end; a token's position counts from its document's first token.
All inputs are finite; a program needn't handle non-finite values.
Results may differ from a plain program's by a relative error of at most 0.025.
Values may be sent and summed in bfloat16 or wider, within the bound.
No kernel may reach another device: no remote copies, remote signals or barrier semaphores. Data moves between devices by JAX's collectives and lax.ppermute only.
A program may use at most 192 MiB of HBM per device.

v0:
```python
import jax
import jax.numpy as jnp
from jax import lax
from jax.sharding import PartitionSpec as P

HD = 256


EPSILON = 1e-06
ROPE_BASE = 1000000.0
MASKED_SCORE = -1e30


def inv_rms(values):
    return lax.rsqrt(jnp.mean(values * values, axis=-1, keepdims=True) + EPSILON)


def rms_back(values, scale_rows, cot_scaled):
    return scale_rows * cot_scaled - values * scale_rows**3 * jnp.mean(
        values * cot_scaled, axis=-1, keepdims=True
    )


def gelu_tanh(values):
    return 0.5 * values * (1.0 + jnp.tanh(0.7978845608028654 * (values + 0.044715 * values**3)))


def rotate(values, cos_table, sin_table):
    middle = values.shape[-1] // 2
    upper_half = values[..., :middle]
    lower_half = values[..., middle:]
    return jnp.concatenate(
        [
            upper_half * cos_table - lower_half * sin_table,
            lower_half * cos_table + upper_half * sin_table,
        ],
        axis=-1,
    )


def rotate_back(values, cos_table, sin_table):
    middle = values.shape[-1] // 2
    upper_half = values[..., :middle]
    lower_half = values[..., middle:]
    return jnp.concatenate(
        [
            upper_half * cos_table + lower_half * sin_table,
            lower_half * cos_table - upper_half * sin_table,
        ],
        axis=-1,
    )


def dot_last(left, right):
    return lax.dot_general(
        left, right, (((1,), (1,)), ((), ())), preferred_element_type=jnp.float32
    )


def dot_first(left, right):
    return lax.dot_general(
        left, right, (((0,), (0,)), ((), ())), preferred_element_type=jnp.float32
    )


def on_device(
    inputs,
    positions,
    norm_gains,
    head_gains,
    attn_split,
    attn_shared,
    ffn_gate_up,
    ffn_down,
    cotangent,
):
    tokens = inputs[0]
    cot_rows = cotangent[0]
    token_pos = positions[0]
    local_len = tokens.shape[0]
    split_all, shared_all, gains_all, gateup_all, down_all = (
        lax.all_gather(attn_split, "fsdp", axis=0, tiled=True),
        lax.all_gather(attn_shared, "fsdp", axis=0, tiled=True),
        lax.all_gather(norm_gains, "fsdp", axis=0, tiled=True),
        lax.all_gather(ffn_gate_up, "fsdp", axis=0, tiled=True),
        lax.all_gather(ffn_down, "fsdp", axis=0, tiled=True),
    )
    gains = gains_all.astype(jnp.float32)
    head_scale = head_gains.astype(jnp.float32)
    model_width = split_all.shape[0]
    query_width = split_all.shape[2]
    heads_local = query_width // HD
    ff_local = gateup_all.shape[2]
    w_query = split_all[:, 0]
    w_output = split_all[:, 1]
    w_keyval = shared_all.reshape(model_width, 2 * HD)
    w_gateup = gateup_all.reshape(model_width, 2 * ff_local)
    score_scale = HD ** (-0.5)
    frequency = ROPE_BASE ** (-2.0 * jnp.arange(HD // 2, dtype=jnp.float32) / HD)
    scale_in = inv_rms(tokens)
    unit_in = tokens * scale_in
    normed_in = (unit_in * gains[:, 0]).astype(jnp.bfloat16)
    queries = jnp.dot(normed_in, w_query, preferred_element_type=jnp.float32).reshape(
        local_len, heads_local, HD
    )
    keyval = jnp.dot(normed_in, w_keyval, preferred_element_type=jnp.float32)
    key_raw = keyval[:, :HD]
    val_raw = keyval[:, HD:]
    scale_q = inv_rms(queries)
    unit_q = queries * scale_q
    scale_k = inv_rms(key_raw)
    unit_k = key_raw * scale_k
    angles = token_pos.astype(jnp.float32)[:, None] * frequency[None, :]
    cos_table = jnp.cos(angles)
    sin_table = jnp.sin(angles)
    query_bf = (
        rotate(unit_q * head_scale[0], cos_table[:, None], sin_table[:, None]) * score_scale
    ).astype(jnp.bfloat16)
    key_bf = rotate(unit_k * head_scale[1], cos_table, sin_table).astype(jnp.bfloat16)
    val_bf = val_raw.astype(jnp.bfloat16)
    keys_all, vals_all = (
        lax.all_gather(key_bf, "ctx", axis=0, tiled=True),
        lax.all_gather(val_bf, "ctx", axis=0, tiled=True),
    )
    query_index = lax.axis_index("ctx") * local_len + jnp.arange(local_len, dtype=jnp.int32)
    key_index = jnp.arange(keys_all.shape[0], dtype=jnp.int32)
    visible = (key_index[None, :] <= query_index[:, None]) & (
        key_index[None, :] >= (query_index - token_pos)[:, None]
    )
    scores = jnp.where(
        visible[None],
        jnp.einsum("chd,kd->hck", query_bf, keys_all, preferred_element_type=jnp.float32),
        MASKED_SCORE,
    )
    row_max = jnp.max(scores, axis=-1, keepdims=True)
    log_total = row_max + jnp.log(jnp.sum(jnp.exp(scores - row_max), axis=-1, keepdims=True))
    probs_bf = jnp.exp(scores - log_total).astype(jnp.bfloat16)
    attended = jnp.einsum("hck,kd->chd", probs_bf, vals_all, preferred_element_type=jnp.float32)
    attended_bf = attended.astype(jnp.bfloat16).reshape(local_len, query_width)
    branch_attn = lax.psum(dot_last(attended_bf, w_output), "tp")
    scale_attn = inv_rms(branch_attn)
    unit_attn = branch_attn * scale_attn
    hidden_in = tokens + unit_attn * gains[:, 1]
    scale_mid = inv_rms(hidden_in)
    unit_mid = hidden_in * scale_mid
    normed_mid = (unit_mid * gains[:, 2]).astype(jnp.bfloat16)
    gate_up = jnp.dot(normed_mid, w_gateup, preferred_element_type=jnp.float32).reshape(
        local_len, 2, ff_local
    )
    gate_pre = gate_up[:, 0]
    up_proj = gate_up[:, 1]
    activated, gelu_grad = jax.vjp(gelu_tanh, gate_pre)
    hidden_bf = (activated * up_proj).astype(jnp.bfloat16)
    branch_ffn = lax.psum(dot_last(hidden_bf, down_all).astype(jnp.bfloat16), "tp").astype(
        jnp.float32
    )
    scale_ffn = inv_rms(branch_ffn)
    unit_ffn = branch_ffn * scale_ffn
    result = hidden_in + unit_ffn * gains[:, 3]
    grad_ffn_bf = rms_back(branch_ffn, scale_ffn, cot_rows * gains[:, 3]).astype(jnp.bfloat16)
    grad_hidden = jnp.dot(grad_ffn_bf, down_all, preferred_element_type=jnp.float32)
    grad_gate = gelu_grad(grad_hidden * up_proj)[0]
    grad_up = grad_hidden * activated
    grad_gateup = (
        jnp.stack([grad_gate, grad_up], axis=1)
        .astype(jnp.bfloat16)
        .reshape(local_len, 2 * ff_local)
    )
    grad_mid_in = dot_last(grad_gateup, w_gateup)
    grad_resid = cot_rows + lax.psum(
        rms_back(hidden_in, scale_mid, gains[:, 2] * grad_mid_in).astype(jnp.bfloat16), "tp"
    ).astype(jnp.float32)
    grad_attn_bf = rms_back(branch_attn, scale_attn, gains[:, 1] * grad_resid).astype(jnp.bfloat16)
    grad_heads = (
        jnp.dot(grad_attn_bf, w_output, preferred_element_type=jnp.float32)
        .astype(jnp.bfloat16)
        .reshape(local_len, heads_local, HD)
    )
    again_scores = jnp.where(
        visible[None],
        jnp.einsum("chd,kd->hck", query_bf, keys_all, preferred_element_type=jnp.float32),
        MASKED_SCORE,
    )
    probs = jnp.exp(again_scores - log_total)
    again_probs_bf = probs.astype(jnp.bfloat16)
    grad_probs = jnp.einsum("chd,kd->hck", grad_heads, vals_all, preferred_element_type=jnp.float32)
    row_delta = jnp.sum(grad_heads.astype(jnp.float32) * attended, axis=-1).T[:, :, None]
    grad_scores_bf = (probs * (grad_probs - row_delta)).astype(jnp.bfloat16)
    grad_qrot = (
        jnp.einsum("hck,kd->chd", grad_scores_bf, keys_all, preferred_element_type=jnp.float32)
        * score_scale
    )
    key_terms = jnp.einsum(
        "hck,chd->kd", grad_scores_bf, query_bf, preferred_element_type=jnp.float32
    )
    val_terms = jnp.einsum(
        "hck,chd->kd", again_probs_bf, grad_heads, preferred_element_type=jnp.float32
    )
    grad_krot, grad_vals = (
        lax.psum_scatter(
            key_terms.astype(jnp.bfloat16), ("ctx", "tp"), scatter_dimension=0, tiled=True
        ).astype(jnp.float32),
        lax.psum_scatter(
            val_terms.astype(jnp.bfloat16), ("ctx", "tp"), scatter_dimension=0, tiled=True
        ).astype(jnp.float32),
    )
    part_len = grad_krot.shape[0]
    part_start = lax.axis_index("tp") * part_len

    def rows_of(array):
        return lax.dynamic_slice_in_dim(array, part_start, part_len, 0)

    grad_qn = rotate_back(grad_qrot, cos_table[:, None], sin_table[:, None])
    grad_q = rms_back(queries, scale_q, head_scale[0] * grad_qn)
    grad_kn = rotate_back(grad_krot, rows_of(cos_table), rows_of(sin_table))
    grad_k = rms_back(rows_of(key_raw), rows_of(scale_k), head_scale[1] * grad_kn)
    grad_q_bf = grad_q.reshape(local_len, query_width).astype(jnp.bfloat16)
    grad_kv_bf = jnp.concatenate([grad_k, grad_vals], axis=1).astype(jnp.bfloat16)
    normed_part = rows_of(normed_in)
    kv_input = lax.dynamic_update_slice_in_dim(
        jnp.zeros((local_len, model_width), jnp.float32),
        dot_last(grad_kv_bf, w_keyval),
        part_start,
        0,
    )
    grad_norm_in = dot_last(grad_q_bf, w_query) + kv_input
    grad_tokens = grad_resid + lax.psum(
        rms_back(tokens, scale_in, gains[:, 0] * grad_norm_in).astype(jnp.bfloat16), "tp"
    ).astype(jnp.float32)
    head_terms = jnp.stack(
        [jnp.sum(unit_q * grad_qn, axis=(0, 1)), jnp.sum(rows_of(unit_k) * grad_kn, axis=0)]
    )
    d_head = lax.psum(head_terms, ("fsdp", "ctx", "tp"))
    shard_rows = attn_split.shape[0]
    split_part = jnp.concatenate(
        [
            dot_first(normed_in, grad_q_bf),
            dot_first(grad_attn_bf, attended_bf),
            dot_first(normed_mid, grad_gateup),
            dot_first(grad_ffn_bf, hidden_bf),
            jnp.sum(unit_attn * grad_resid, axis=0)[:, None],
            jnp.sum(unit_ffn * cot_rows, axis=0)[:, None],
        ],
        axis=1,
    )
    shared_part = jnp.concatenate(
        [
            dot_first(normed_part, grad_kv_bf),
            jnp.sum(unit_in * grad_norm_in, axis=0)[:, None],
            jnp.sum(unit_mid * grad_mid_in, axis=0)[:, None],
        ],
        axis=1,
    )
    summed = lax.psum_scatter(
        jnp.concatenate([split_part, shared_part], axis=1).astype(jnp.bfloat16),
        "fsdp",
        scatter_dimension=0,
        tiled=True,
    ).astype(jnp.float32)
    summed = lax.psum(summed.astype(jnp.bfloat16), "ctx").astype(jnp.float32)
    split_cols = 2 * query_width + 3 * ff_local + 2
    shared_sum = lax.psum(summed[:, split_cols:].astype(jnp.bfloat16), "tp").astype(jnp.float32)
    d_split = jnp.stack([summed[:, :query_width], summed[:, query_width : 2 * query_width]], axis=1)
    offset = 2 * query_width
    d_gateup = summed[:, offset : offset + 2 * ff_local].reshape(shard_rows, 2, ff_local)
    d_down = summed[:, offset + 2 * ff_local : offset + 3 * ff_local]
    d_shared = shared_sum[:, : 2 * HD].reshape(shard_rows, 2, HD)
    d_gains = jnp.stack(
        [
            shared_sum[:, 2 * HD],
            summed[:, split_cols - 2],
            shared_sum[:, 2 * HD + 1],
            summed[:, split_cols - 1],
        ],
        axis=1,
    )
    return (result[None], grad_tokens[None], d_gains, d_head, d_split, d_shared, d_gateup, d_down)


def solution(mesh):
    in_specs = (
        P("fsdp", "ctx", None),
        P("fsdp", "ctx"),
        P("fsdp", None),
        P(),
        P("fsdp", None, "tp"),
        P("fsdp", None, None),
        P("fsdp", None, "tp"),
        P("fsdp", "tp"),
        P("fsdp", "ctx", None),
    )
    out_specs = (
        P("fsdp", "ctx", None),
        P("fsdp", "ctx", None),
        P("fsdp", None),
        P(),
        P("fsdp", None, "tp"),
        P("fsdp", None, None),
        P("fsdp", None, "tp"),
        P("fsdp", "tp"),
    )
    return jax.shard_map(
        on_device, mesh=mesh, in_specs=in_specs, out_specs=out_specs, check_vma=False
    )
```

profile of v0, /device:TPU:1, one launch (start us, length us, event | category | flops | bytes accessed | tf_op | source)
XLA Modules:
  0.0 1127.7 jit_solution(15583414969608106842)
XLA Ops:
  9.8 27.6 %all-gather = bf16[8,144,4]{1,2,0:T(4,128)(2,1)S(1)} all-gather(bf16[1,144,4]{1,2,0:T(4,128)(2,1)} %bitcast.204), channel_id=1, replica_groups=mesh['fsdp'=8,'ctx'=8,'tp'=2] {'fsdp'}, dimensions={0}, use_global_device_ids=true | all-gather | bytes 10368 | tf_op jit(solution)/shard_map/all_gather | solution.py:84
  40.3 18.4 %all-gather.6.cloned.1.call-done = bf16[1152,2,256]{2,1,0:T(2,128)(2,1)} async-done(((bf16[144,2,256]{2,1,0:T(2,128)(2,1)}), bf16[1152,2,256]{2,1,0:T(2,128)(2,1)}) %all-gather.6.cloned.1.call-update) | async-done | bytes 1179664 | tf_op jit(solution)/shard_map/all_gather | solution.py:83
  62.4 15.9 %all_gather.24 = bf16[1024,256]{1,0:T(8,128)(2,1)S(1)} all-gather(bf16[128,256]{1,0:T(8,128)(2,1)S(1)} %pad_maximum_fusion.2), channel_id=1, replica_groups=mesh['fsdp'=8,'ctx'=8,'tp'=2] {'ctx'}, dimensions={0}, use_global_device_ids=true | all-gather | bytes 589824 | tf_op jit(solution)/shard_map/all_gather | solution.py:122
  78.3 13.1 %all_gather.23 = bf16[1024,256]{1,0:T(8,128)(2,1)S(1)} all-gather(bf16[128,256]{1,0:T(8,128)(2,1)S(1)} %slice.211), channel_id=1, replica_groups=mesh['fsdp'=8,'ctx'=8,'tp'=2] {'ctx'}, dimensions={0}, use_global_device_ids=true | all-gather | bytes 589824 | tf_op jit(solution)/shard_map/all_gather | solution.py:123
  91.4 26.0 %all-gather.8.cloned.1.call-done = bf16[1152,2,512]{2,0,1:T(8,128)(2,1)} async-done(((bf16[144,2,512]{2,0,1:T(8,128)(2,1)}), bf16[1152,2,512]{2,0,1:T(8,128)(2,1)}) %all-gather.8.cloned.1.call-update) | async-done | bytes 2359312 | tf_op jit(solution)/shard_map/all_gather | solution.py:82
  117.4 2.4 slice_bitcast_fusion.5
  129.5 32.9 %all-reduce.7.cloned.1.call-done = f32[128,1152]{1,0:T(8,128)} async-done(((f32[128,1152]{1,0:T(8,128)}), f32[128,1152]{1,0:T(8,128)}) %all-reduce.7.cloned.1.call-update) | async-done | bytes 589840 | tf_op jit(solution)/shard_map/psum | solution.py:140
  164.2 2.0 multiply_reduce_fusion.5
  166.8 173.6 %all-gather.10.cloned.1.call-done = bf16[1152,2,3456]{2,0,1:T(8,128)(2,1)} async-done(((bf16[144,2,3456]{2,0,1:T(8,128)(2,1)}), bf16[1152,2,3456]{2,0,1:T(8,128)(2,1)}) %all-gather.10.cloned.1.call-update) | async-done | bytes 15925264 | tf_op jit(solution)/shard_map/all_gather | solution.py:85
  340.4 21.6 %copy.89 = bf16[1152,2,3456]{0,2,1:T(8,128)(2,1)} copy(bf16[1152,2,3456]{2,0,1:T(8,128)(2,1)} %all-gather.10.cloned.1.call-done) | data formatting | bytes 31850496 | tf_op jit(solution)/shard_map/all_gather | solution.py:85
  362.0 10.2 fusion
  373.8 69.5 %all-gather.12.cloned.1.call-done = bf16[1152,3456]{1,0:T(8,128)(2,1)} async-done(((bf16[144,3456]{1,0:T(8,128)(2,1)}), bf16[1152,3456]{1,0:T(8,128)(2,1)}) %all-gather.12.cloned.1.call-update) | async-done | bytes 7962640 | tf_op jit(solution)/shard_map/all_gather | solution.py:86
  443.3 6.7 convolution_convert_fusion.5
  451.6 26.9 %all-reduce.9.cloned.1.call-done = bf16[128,1152]{1,0:T(8,128)(2,1)} async-done(((bf16[128,1152]{1,0:T(8,128)(2,1)}), bf16[128,1152]{1,0:T(8,128)(2,1)}) %all-reduce.9.cloned.1.call-update) | async-done | bytes 294928 | tf_op jit(solution)/shard_map/psum | solution.py:154
  479.7 1.9 fusion.27
  481.6 5.8 fusion.10
  488.9 2.2 copy.97
  491.2 11.0 multiply_reduce_fusion
  505.6 9.6 convolution_convert_fusion
  515.3 5.6 convolution_convert_fusion.1
  520.9 15.8 %all-reduce.11.cloned.1.call-done = bf16[128,1152]{1,0:T(8,128)(2,1)} async-done(((bf16[128,1152]{1,0:T(8,128)(2,1)}), bf16[128,1152]{1,0:T(8,128)(2,1)}) %all-reduce.11.cloned.1.call-update) | async-done | bytes 294928 | tf_op jit(solution)/shard_map/psum | solution.py:170
  550.4 2.0 fusion.17
  552.4 53.1 %reduce-scatter.4.cloned.1.call-done = bf16[64,256]{1,0:T(8,128)(2,1)} async-done(((bf16[1024,256]{1,0:T(8,128)(2,1)}), bf16[64,256]{1,0:T(8,128)(2,1)}) %reduce-scatter.4.cloned.1.call-update) | async-done | bytes 32784 | tf_op jit(solution)/shard_map/reduce_scatter | solution.py:200
  610.1 58.7 %reduce-scatter.6.cloned.1.call-done = bf16[64,256]{1,0:T(8,128)(2,1)} async-done(((bf16[1024,256]{1,0:T(8,128)(2,1)}), bf16[64,256]{1,0:T(8,128)(2,1)}) %reduce-scatter.6.cloned.1.call-update) | async-done | bytes 32784 | tf_op jit(solution)/shard_map/reduce_scatter | solution.py:203
  673.3 47.7 %concatenate.26 = bf16[1152,11908]{1,0:T(8,128)(2,1)} concatenate(bf16[1152,512]{1,0:T(8,128)(2,1)S(1)} %copy.99, bf16[1152,512]{1,0:T(8,128)(2,1)S(1)} %copy-done.21, bf16[1152,6912]{1,0:T(8,128)(2,1)} %convolution_convert_fusion, bf16[1152,3456]{1,0:T(8,128)(2,1)} %convolution_convert_fusion.1, bf16[1152,1]{1,0:T(8,128)(2,1)} %broadcast_in_dim.40, ...), dimensions={1} | concatenate | bytes 54872064 | tf_op jit(solution)/shard_map/concatenate | solution.py:255
  721.1 283.2 %reduce-scatter.8.cloned.1.call-done = bf16[144,11908]{1,0:T(8,128)(2,1)} async-done(((bf16[1152,11908]{1,0:T(8,128)(2,1)}), bf16[144,11908]{1,0:T(8,128)(2,1)}) %reduce-scatter.8.cloned.1.call-update) | async-done | bytes 3429520 | tf_op jit(solution)/shard_map/reduce_scatter | solution.py:254
  1004.4 67.0 %psum.55 = f32[2,256]{1,0:T(2,128)} all-reduce(f32[2,256]{1,0:T(2,128)S(1)} %pad_maximum_fusion.8), channel_id=1, replica_groups=mesh['fsdp'=8,'ctx'=8,'tp'=2] {'fsdp','ctx','tp'}, use_global_device_ids=true, to_apply=%region_30.31 | all-reduce | flops 512 | bytes 4096 | tf_op jit(solution)/shard_map/psum | solution.py:233
  1072.3 5.1 all-reduce.13.cloned.1.call-done
  1077.4 1.7 slice.148
  1080.2 3.8 slice.156
  1084.1 5.8 reshape.330
  1093.1 23.3 %all-reduce.15.cloned.1.call-done = (bf16[144,514]{1,0:T(8,128)(2,1)}, bf16[128,1152]{1,0:T(8,128)(2,1)}) async-done(((bf16[144,514]{1,0:T(8,128)(2,1)}, bf16[128,1152]{1,0:T(8,128)(2,1)}), (bf16[144,514]{1,0:T(8,128)(2,1)}, bf16[128,1152]{1,0:T(8,128)(2,1)})) %all-reduce.15.cloned.1.call-update) | async-done | bytes 442960 | tf_op jit(solution)/shard_map/psum | solution.py:262
  (273 shorter events, 62.1 us)
Async XLA Ops:
  7.2 33.0 %copy-start.6 = (f32[1,128,1152]{2,1,0:T(8,128)S(1)}, f32[1,128,1152]{2,1,0:T(8,128)}, u32[]{:S(2)}) copy-start(f32[1,128,1152]{2,1,0:T(8,128)} %param.9) | copy-start | bytes 1769476
  7.2 32.2 %copy-start.77 = (s32[1,128]{1,0:T(1,128)S(1)}, s32[1,128]{1,0:T(1,128)}, u32[]{:S(2)}) copy-start(s32[1,128]{1,0:T(1,128)} %param.10) | copy-start | bytes 1540
  7.2 32.8 %copy-start.68 = (bf16[2,256]{1,0:T(2,128)(2,1)S(1)}, bf16[2,256]{1,0:T(2,128)(2,1)}, u32[]{:S(2)}) copy-start(bf16[2,256]{1,0:T(2,128)(2,1)} %param.12) | copy-start | bytes 3076
  7.2 51.5 %all-gather.6.cloned.1.call-start = ((), (), s32[]{:S(2)}) async-start(), calls=%async_computation.3 | async-start | bytes 1327104 | tf_op jit(solution)/shard_map/all_gather | solution.py:83
  7.9 109.5 %all-gather.8.cloned.1.call-start = ((), (), s32[]{:S(2)}) async-start(), calls=%async_computation.4 | async-start | bytes 2654208 | tf_op jit(solution)/shard_map/all_gather | solution.py:82
  9.7 152.7 %all-reduce.7.cloned.1.call-start = ((), (), s32[]{:S(2)}) async-start(), calls=%async_computation.5 | async-start | bytes 1179648 | tf_op jit(solution)/shard_map/psum | solution.py:140
  38.1 126.1 %copy-start.46 = (f32[1152]{0:T(1024)}, f32[1152]{0:T(1024)S(1)}, u32[]{:S(2)}) copy-start(f32[1152]{0:T(1024)S(1)} %get-tuple-element.54) | copy-start | bytes 13828
  40.0 82.7 %copy-start.56 = (f32[1,256]{1,0:T(1,128)}, f32[1,256]{1,0:T(1,128)S(1)}, u32[]{:S(2)}) copy-start(f32[1,256]{1,0:T(1,128)S(1)} %get-tuple-element.91) | copy-start | bytes 3076
  40.3 81.2 %copy-start.19 = (bf16[1,128,1152]{2,1,0:T(8,128)(2,1)}, bf16[1,128,1152]{2,1,0:T(8,128)(2,1)S(1)}, u32[]{:S(2)}) copy-start(bf16[1,128,1152]{2,1,0:T(8,128)(2,1)S(1)} %multiply_convert_fusion.2) | copy-start | bytes 884740
  61.3 58.5 %copy-start.73 = (f32[128]{0:T(128)}, f32[128]{0:T(128)S(1)}, u32[]{:S(2)}) copy-start(f32[128]{0:T(128)S(1)} %add_rsqrt_fusion.4) | copy-start | bytes 1540
  62.3 60.4 %copy-start.39 = (f32[128,128]{1,0:T(8,128)}, f32[128,128]{1,0:T(8,128)S(1)}, u32[]{:S(2)}) copy-start(f32[128,128]{1,0:T(8,128)S(1)} %get-tuple-element.87) | copy-start | bytes 196612
  62.3 60.4 %copy-start.41 = (f32[128,128]{1,0:T(8,128)}, f32[128,128]{1,0:T(8,128)S(1)}, u32[]{:S(2)}) copy-start(f32[128,128]{1,0:T(8,128)S(1)} %get-tuple-element.88) | copy-start | bytes 196612
  78.3 44.5 %copy-start.17 = (bf16[1024,256]{1,0:T(8,128)(2,1)}, bf16[1024,256]{1,0:T(8,128)(2,1)S(1)}, u32[]{:S(2)}) copy-start(bf16[1024,256]{1,0:T(8,128)(2,1)S(1)} %all_gather.24) | copy-start | bytes 1572868
  91.4 32.1 %copy-start.15 = (bf16[1024,256]{1,0:T(8,128)(2,1)}, bf16[1024,256]{1,0:T(8,128)(2,1)S(1)}, u32[]{:S(2)}) copy-start(bf16[1024,256]{1,0:T(8,128)(2,1)S(1)} %all_gather.23) | copy-start | bytes 1572868
  127.3 213.1 %all-gather.10.cloned.1.call-start = ((), (), s32[]{:S(2)}) async-start(), calls=%async_computation.6 | async-start | bytes 17915904 | tf_op jit(solution)/shard_map/all_gather | solution.py:85
  128.9 314.4 %all-gather.12.cloned.1.call-start = ((), (), s32[]{:S(2)}) async-start(), calls=%async_computation.7 | async-start | bytes 8957952 | tf_op jit(solution)/shard_map/all_gather | solution.py:86
  129.5 349.0 %all-reduce.9.cloned.1.call-start = ((), (), s32[]{:S(2)}) async-start(), calls=%async_computation.8 | async-start | bytes 589824 | tf_op jit(solution)/shard_map/psum | solution.py:154
  164.2 197.8 %copy-start.61 = (f32[128]{0:T(128)}, f32[128]{0:T(128)S(1)}, u32[]{:S(2)}) copy-start(f32[128]{0:T(128)S(1)} %get-tuple-element.96) | copy-start | bytes 1540
  450.0 86.7 %all-reduce.11.cloned.1.call-start = ((), (), s32[]{:S(2)}) async-start(), calls=%async_computation.9 | async-start | bytes 589824 | tf_op jit(solution)/shard_map/psum | solution.py:170
  505.3 100.1 %reduce-scatter.4.cloned.1.call-start = ((), (), s32[]{:S(2)}) async-start(), calls=%async_computation.10 | async-start | bytes 557056 | tf_op jit(solution)/shard_map/reduce_scatter | solution.py:200
  543.1 125.7 %reduce-scatter.6.cloned.1.call-start = ((), (), s32[]{:S(2)}) async-start(), calls=%async_computation.11 | async-start | bytes 557056 | tf_op jit(solution)/shard_map/reduce_scatter | solution.py:203
  550.3 56.7 %copy-start.55 = (f32[1,256]{1,0:T(1,128)S(1)}, f32[1,256]{1,0:T(1,128)}, u32[]{:S(2)}) copy-start(f32[1,256]{1,0:T(1,128)} %copy-done.54) | copy-start | bytes 3076
  550.3 118.5 %copy-start.9 = (bf16[144,8,2,256]{3,1,2,0:T(8,128)(2,1)S(1)}, bf16[144,8,2,256]{3,1,2,0:T(8,128)(2,1)}, u32[]{:S(2)}) copy-start(bf16[144,8,2,256]{3,1,2,0:T(8,128)(2,1)} %copy-done.8) | copy-start | bytes 3538948
  550.3 119.8 %copy-start.7 = (f32[1,128,1152]{2,1,0:T(8,128)S(1)}, f32[1,128,1152]{2,1,0:T(8,128)}, u32[]{:S(2)}) copy-start(f32[1,128,1152]{2,1,0:T(8,128)} %param.9) | copy-start | bytes 1769476
  550.3 119.8 %copy-start.64 = (f32[128]{0:T(128)S(1)}, f32[128]{0:T(128)}, u32[]{:S(2)}) copy-start(f32[128]{0:T(128)} %copy-done.63) | copy-start | bytes 1540
  550.4 453.9 %reduce-scatter.8.cloned.1.call-start = ((), (), s32[]{:S(2)}) async-start(), calls=%async_computation.12 | async-start | bytes 31186944 | tf_op jit(solution)/shard_map/reduce_scatter | solution.py:254
  721.0 283.4 %copy-start.66 = (f32[256]{0:T(256)S(1)}, f32[256]{0:T(256)}, u32[]{:S(2)}) copy-start(f32[256]{0:T(256)} %get-tuple-element.48) | copy-start | bytes 3076
  721.0 283.4 %copy-start.67 = (f32[256]{0:T(256)S(1)}, f32[256]{0:T(256)}, u32[]{:S(2)}) copy-start(f32[256]{0:T(256)} %get-tuple-element.50) | copy-start | bytes 3076
  721.0 350.4 %copy-start.76 = (f32[128]{0:T(128)S(1)}, f32[128]{0:T(128)}, u32[]{:S(2)}) copy-start(f32[128]{0:T(128)} %get-tuple-element.47) | copy-start | bytes 1540
  721.0 350.4 %copy-start.74 = (f32[128]{0:T(128)S(1)}, f32[128]{0:T(128)}, u32[]{:S(2)}) copy-start(f32[128]{0:T(128)} %get-tuple-element.93) | copy-start | bytes 1540
  721.0 356.4 %all-reduce.13.cloned.1.call-start = ((), (), s32[]{:S(2)}) async-start(), calls=%async_computation.13 | async-start | bytes 6930432 | tf_op jit(solution)/shard_map/psum | solution.py:260
  1004.3 112.1 %all-reduce.15.cloned.1.call-start = ((), (), s32[]{:S(2)}) async-start(), calls=%async_computation.14 | async-start | bytes 958464 | tf_op jit(solution)/shard_map/psum | solution.py:262
  (59 other events, 404.1 us)
Sparse Core Ops, SparseCore 0:
  10.3 48.2 all-gather.5
  61.6 55.7 all-gather.7
  127.5 34.9 all-reduce.6
  165.2 175.1 all-gather.9
  342.6 100.6 all-gather.11
  450.2 28.3 all-reduce.8
  505.5 31.2 all-reduce.10
  543.2 62.1 reduce-scatter.3
  608.4 60.3 reduce-scatter.5
  721.1 283.1 reduce-scatter.7
  1006.7 70.6 all-reduce.12
  1080.4 35.9 all-reduce.14
where the time goes:
time: 1130 us
  waiting for transfers between devices  788 us (70%)
  blocking collectives  124 us (11%)
  local copies, waits for them, and re-layouts  109 us (10%)
  matrix products  62.7 us (6%)
  other arithmetic  28 us (2%)
  between operations  15.2 us (1%)
    reduce_scatter x1, waiting for transfers between devices, on_device(): lax.psum_scatter(jnp.concatenate([split_part, shared_part], axis=1).astyp...  283 us
    all_gather x1, waiting for transfers between devices, on_device(): lax.all_gather(ffn_gate_up, 'fsdp', axis=0, tiled=True)  174 us
    all_gather x1, waiting for transfers between devices, on_device(): lax.all_gather(ffn_down, 'fsdp', axis=0, tiled=True)  69.5 us
    psum x1, blocking collectives, on_device(): d_head = lax.psum(head_terms, ('fsdp', 'ctx', 'tp'))  67 us
    reduce_scatter x1, waiting for transfers between devices, on_device(): lax.psum_scatter(val_terms.astype(jnp.bfloat16), ('ctx', 'tp'), scatter_d...  58.7 us
    reduce_scatter x1, waiting for transfers between devices, on_device(): lax.psum_scatter(key_terms.astype(jnp.bfloat16), ('ctx', 'tp'), scatter_d...  53.1 us
    concatenate x1, local copies, waits for them, and re-layouts, on_device(): jnp.concatenate([split_part, shared_part], axis=1).astype(jnp.bfloat16)  47.7 us
    psum x1, waiting for transfers between devices, on_device(): branch_attn = lax.psum(dot_last(attended_bf, w_output), 'tp')  32.9 us
  transfers between devices with their start and end apart: 12, of which 12 were waited for; matrix products, arithmetic and copies ran while one was open for 8% of the time, Pallas kernels for 0%

commit v1 on v0

v1 whole, which is shorter than its diff:
```python
import jax
import jax.numpy as jnp
from jax import lax
from jax.sharding import Mesh, PartitionSpec as P

HD = 256
EPSILON = 1e-06
ROPE_BASE = 1000000.0
MASKED_SCORE = -1e30
SIZE = {"z": 4, "xh": 2, "y": 4, "core": 2, "tp": 2}
BF = jnp.bfloat16
F32 = jnp.float32


def inv_rms(values):
    return lax.rsqrt(jnp.mean(values * values, axis=-1, keepdims=True) + EPSILON)


def rms_back(values, scale_rows, cot_scaled):
    return scale_rows * cot_scaled - values * scale_rows**3 * jnp.mean(
        values * cot_scaled, axis=-1, keepdims=True
    )


def rotate(values, cos_table, sin_table):
    middle = values.shape[-1] // 2
    upper_half = values[..., :middle]
    lower_half = values[..., middle:]
    return jnp.concatenate(
        [
            upper_half * cos_table - lower_half * sin_table,
            lower_half * cos_table + upper_half * sin_table,
        ],
        axis=-1,
    )


def rotate_back(values, cos_table, sin_table):
    return rotate(values, cos_table, -sin_table)


def dot(left, right):
    return jnp.dot(left, right, preferred_element_type=F32)


def dot_last(left, right):
    return lax.dot_general(left, right, (((1,), (1,)), ((), ())), preferred_element_type=F32)


def dot_first(left, right):
    return lax.dot_general(left, right, (((0,), (0,)), ((), ())), preferred_element_type=F32)


def send(array, axis, shift):
    n = SIZE[axis]
    return lax.ppermute(array, axis, [(i, (i + shift) % n) for i in range(n)])


def gather_rows(shard, z, xh):
    rows, cols = shard.shape
    other = send(shard, "xh", 1)
    pair = jnp.where(
        xh == 0, jnp.concatenate([shard, other], 0), jnp.concatenate([other, shard], 0)
    )
    whole = jnp.zeros((4, 2 * rows, cols), shard.dtype)
    whole = lax.dynamic_update_slice(whole, pair[None], (z, 0, 0))
    for k in range(1, 4):
        whole = lax.dynamic_update_slice(
            whole, send(pair, "z", k)[None], (lax.rem(z + 4 - k, 4), 0, 0)
        )
    return whole.reshape(8 * rows, cols)


def scatter_rows(whole, z, xh):
    total, cols = whole.shape
    rows = total // 8
    blocks = whole.astype(BF).reshape(4, 2 * rows, cols)
    pair = lax.dynamic_index_in_dim(blocks, z, 0, False).astype(F32)
    for k in range(1, 4):
        block = lax.dynamic_index_in_dim(blocks, lax.rem(z + 4 - k, 4), 0, False)
        pair = pair + send(block, "z", -k).astype(F32)
    pair = pair.astype(BF).reshape(2, rows, cols)
    away = lax.dynamic_index_in_dim(pair, 1 - xh, 0, False)
    own = lax.dynamic_index_in_dim(pair, xh, 0, False)
    return own.astype(F32) + send(away, "xh", 1).astype(F32)


def gather_tokens(block):
    mine = jnp.concatenate([block] + [send(block, "y", k) for k in range(1, 4)], 0)
    return jnp.concatenate([mine, send(mine, "core", 1)], 0)


def pair_sum(array):
    rounded = array.astype(BF)
    return rounded.astype(F32) + send(rounded, "tp", 1).astype(F32)


def scatter_tokens(partial):
    half = partial.shape[0] // 2
    local = half // 4
    away = send(partial[half:].astype(BF), "core", 1)
    mine = partial[:half] + away.astype(F32)
    rounded = mine.astype(BF)
    total = mine[:local]
    for k in range(1, 4):
        total = total + send(rounded[k * local : (k + 1) * local], "y", -k).astype(F32)
    return pair_sum(total)


def ring_sum(array):
    got = [send(array, "y", k).astype(F32) for k in range(1, 4)]
    return (array.astype(F32) + got[1]) + (got[0] + got[2])


def small_sum(array):
    array = array + send(array, "core", 1)
    array = array + send(array, "tp", 1)
    array = array + send(array, "xh", 1)
    for axis in ("y", "z"):
        got = [send(array, axis, k) for k in range(1, 4)]
        array = (array + got[1]) + (got[0] + got[2])
    return array


def swap_halves(array):
    rows, cols = array.shape
    half = 128
    parts = array.reshape(rows // (2 * half), 2, half, cols)
    return jnp.concatenate([parts[:, 1:], parts[:, :1]], 1).reshape(rows, cols)


def on_device(
    inputs,
    positions,
    norm_gains,
    head_gains,
    attn_split,
    attn_shared,
    ffn_gate_up,
    ffn_down,
    cotangent,
):
    z, xh, y, core, tp = (lax.axis_index(a) for a in ("z", "xh", "y", "core", "tp"))
    first = core == 0
    tokens = inputs[0]
    cot_rows = cotangent[0]
    local_len, model_width = tokens.shape
    shard_rows = attn_split.shape[0]
    ff_local = ffn_gate_up.shape[2] // 8
    ff_pad = 512
    place = y * 2 + core

    wq_shard = lax.dynamic_slice(attn_split, (0, 0, core * HD), (shard_rows, 1, HD))[:, 0]
    wo_shard = lax.dynamic_slice(attn_split, (0, 1, core * HD), (shard_rows, 1, HD))[:, 0]
    wkv_shard = lax.dynamic_index_in_dim(attn_shared, core, 1, False)
    gains_shard = jnp.pad(norm_gains, ((0, 0), (0, 124)))
    attn_all = gather_rows(jnp.concatenate([wq_shard, wkv_shard, gains_shard], 1), z, xh)
    gu_shard = lax.dynamic_slice(
        ffn_gate_up, (0, 0, place * ff_local), (shard_rows, 2, ff_local)
    )
    down_shard = lax.dynamic_slice(ffn_down, (0, place * ff_local), (shard_rows, ff_local))

    def padded(array):
        return jnp.pad(array, ((0, 0), (0, ff_pad - ff_local)))

    ffn_all = gather_rows(
        jnp.concatenate(
            [wo_shard, padded(gu_shard[:, 0]), padded(gu_shard[:, 1]), padded(down_shard)], 1
        ),
        z,
        xh,
    )
    w_qkv = attn_all[:, : 2 * HD]
    gains = attn_all[:, 2 * HD : 2 * HD + 4].astype(F32).T
    w_out = ffn_all[:, :HD]
    w_gateup = ffn_all[:, HD : HD + 2 * ff_pad]
    w_down = ffn_all[:, HD + 2 * ff_pad :]

    head_scale = head_gains.astype(F32)
    score_scale = HD ** (-0.5)
    frequency = ROPE_BASE ** (-2.0 * jnp.arange(HD // 2, dtype=F32) / HD)
    own_pos = positions.astype(F32)
    chip_pos = jnp.concatenate([own_pos, send(own_pos, "core", 1)], 1)[0]
    angles = chip_pos[:, None] * frequency[None, :]
    cos_table = jnp.cos(angles)
    sin_table = jnp.sin(angles)

    scale_in = inv_rms(tokens)
    unit_in = tokens * scale_in
    normed_own = (unit_in * gains[0]).astype(BF)
    normed_in = jnp.concatenate([normed_own, send(normed_own, "core", 1)], 0)
    qkv = dot(normed_in, w_qkv)
    queries = qkv[:, :HD]
    kv_raw = qkv[:, HD:]
    scale_q = inv_rms(queries)
    unit_q = queries * scale_q
    scale_k = inv_rms(kv_raw)
    unit_k = kv_raw * scale_k
    query_bf = (rotate(unit_q * head_scale[0], cos_table, sin_table) * score_scale).astype(BF)
    kv_bf = jnp.where(first, rotate(unit_k * head_scale[1], cos_table, sin_table), kv_raw).astype(
        BF
    )
    kv_mine = jnp.concatenate([kv_bf] + [send(kv_bf, "y", k) for k in range(1, 4)], 0)
    kv_other = swap_halves(send(kv_mine, "core", 1))
    keys = jnp.where(first, kv_mine, kv_other)
    vals = jnp.where(first, kv_other, kv_mine)

    chip_len = 2 * local_len
    seq_len = 4 * chip_len
    q_iota = jnp.arange(chip_len, dtype=jnp.int32)
    q_core = lax.rem(core + q_iota // local_len, 2)
    query_index = y * chip_len + q_core * local_len + lax.rem(q_iota, local_len)
    k_iota = jnp.arange(seq_len, dtype=jnp.int32)
    k_core = lax.rem(core + k_iota // local_len, 2)
    key_index = (
        lax.rem(y + 4 - k_iota // chip_len, 4) * chip_len
        + k_core * local_len
        + lax.rem(k_iota, local_len)
    )
    begin = query_index - chip_pos.astype(jnp.int32)
    visible = (key_index[None, :] <= query_index[:, None]) & (key_index[None, :] >= begin[:, None])
    scores = jnp.where(visible, dot_last(query_bf, keys), MASKED_SCORE)
    row_max = jnp.max(scores, axis=-1, keepdims=True)
    log_total = row_max + jnp.log(jnp.sum(jnp.exp(scores - row_max), axis=-1, keepdims=True))
    probs = jnp.exp(scores - log_total)
    probs_bf = probs.astype(BF)
    attended = dot(probs_bf, vals)
    attended_bf = attended.astype(BF)

    def chip_scatter(partial):
        away = send(partial[local_len:].astype(BF), "core", 1)
        return pair_sum(partial[:local_len] + away.astype(F32))

    branch_attn = chip_scatter(dot_last(attended_bf, w_out))
    scale_attn = inv_rms(branch_attn)
    unit_attn = branch_attn * scale_attn
    hidden_in = tokens + unit_attn * gains[1]
    scale_mid = inv_rms(hidden_in)
    unit_mid = hidden_in * scale_mid
    normed_mid = gather_tokens((unit_mid * gains[2]).astype(BF))

    gate_up = dot(normed_mid, w_gateup)
    gate_pre = gate_up[:, :ff_pad]
    up_proj = gate_up[:, ff_pad:]
    cube = 0.7978845608028654
    tanh_part = jnp.tanh(cube * (gate_pre + 0.044715 * gate_pre**3))
    activated = 0.5 * gate_pre * (1.0 + tanh_part)
    slope = 0.5 * (1.0 + tanh_part) + 0.5 * gate_pre * (1.0 - tanh_part * tanh_part) * cube * (
        1.0 + 3.0 * 0.044715 * gate_pre * gate_pre
    )
    hidden_bf = (activated * up_proj).astype(BF)
    branch_ffn = scatter_tokens(dot_last(hidden_bf, w_down))
    scale_ffn = inv_rms(branch_ffn)
    unit_ffn = branch_ffn * scale_ffn
    result = hidden_in + unit_ffn * gains[3]
    grad_ffn = gather_tokens(rms_back(branch_ffn, scale_ffn, cot_rows * gains[3]).astype(BF))
    grad_hidden = dot(grad_ffn, w_down)
    grad_gateup = jnp.concatenate(
        [grad_hidden * up_proj * slope, grad_hidden * activated], 1
    ).astype(BF)
    grad_mid = scatter_tokens(dot_last(grad_gateup, w_gateup))
    d_ffn = scatter_rows(
        jnp.concatenate([dot_first(normed_mid, grad_gateup), dot_first(grad_ffn, hidden_bf)], 1),
        z,
        xh,
    ).astype(BF)

    grad_resid = cot_rows + rms_back(hidden_in, scale_mid, gains[2] * grad_mid)
    grad_attn_own = rms_back(branch_attn, scale_attn, gains[1] * grad_resid).astype(BF)
    grad_attn = jnp.concatenate([grad_attn_own, send(grad_attn_own, "core", 1)], 0)
    grad_heads = dot(grad_attn, w_out).astype(BF)
    grad_probs = dot_last(grad_heads, vals)
    row_delta = jnp.sum(grad_heads.astype(F32) * attended, axis=-1, keepdims=True)
    grad_scores = (probs * (grad_probs - row_delta)).astype(BF)
    grad_qrot = dot(grad_scores, keys) * score_scale
    key_terms = dot_first(grad_scores, query_bf)
    val_terms = dot_first(probs_bf, grad_heads)
    kv_away = swap_halves(jnp.where(first, val_terms, key_terms).astype(BF))
    kv_terms = jnp.where(first, key_terms, val_terms) + send(kv_away, "core", 1).astype(F32)
    kv_rounded = kv_terms.astype(BF)
    kv_total = kv_terms[:chip_len]
    for k in range(1, 4):
        kv_total = kv_total + send(
            kv_rounded[k * chip_len : (k + 1) * chip_len], "y", -k
        ).astype(F32)
    grad_kvrot = pair_sum(kv_total)

    grad_qn = rotate_back(grad_qrot, cos_table, sin_table)
    grad_q_bf = rms_back(queries, scale_q, head_scale[0] * grad_qn).astype(BF)
    grad_kn = rotate_back(grad_kvrot, cos_table, sin_table)
    grad_k = rms_back(kv_raw, scale_k, head_scale[1] * grad_kn)
    grad_kv_bf = jnp.where(first, grad_k, grad_kvrot).astype(BF)
    d_qkv = dot_first(normed_in, jnp.concatenate([grad_q_bf, grad_kv_bf], 1))
    d_out = dot_first(grad_attn, attended_bf)
    d_attn = ring_sum(scatter_rows(jnp.concatenate([d_qkv, d_out], 1), z, xh).astype(BF))
    grad_norm_in = chip_scatter(
        dot_last(jnp.concatenate([grad_q_bf, grad_kv_bf * 0.5], 1), w_qkv)
    )
    grad_tokens = grad_resid + rms_back(tokens, scale_in, gains[0] * grad_norm_in)

    only_first = jnp.where(first, 0.5, 0.0)
    head_row = jnp.concatenate(
        [
            jnp.sum(unit_q * grad_qn, axis=0),
            only_first * jnp.sum(unit_k * grad_kn, axis=0),
            jnp.zeros((model_width - 2 * HD,), F32),
        ]
    )
    gain_rows = [
        jnp.sum(unit_in * grad_norm_in, axis=0),
        jnp.sum(unit_attn * grad_resid, axis=0),
        jnp.sum(unit_mid * grad_mid, axis=0),
        jnp.sum(unit_ffn * cot_rows, axis=0),
    ]
    small = small_sum(jnp.stack([0.5 * r for r in gain_rows] + [head_row]))
    d_head = small[4, : 2 * HD].reshape(2, HD)
    d_gains = lax.dynamic_slice(small, (0, (z * 2 + xh) * shard_rows), (4, shard_rows)).T

    d_attn_bf = d_attn.astype(BF)
    d_other = send(d_attn_bf, "core", 1)
    by_core = jnp.where(
        first, jnp.stack([d_attn_bf, d_other], 1), jnp.stack([d_other, d_attn_bf], 1)
    ).astype(F32)
    d_split = jnp.stack(
        [
            by_core[:, :, :HD].reshape(shard_rows, 2 * HD),
            by_core[:, :, 2 * HD :].reshape(shard_rows, 2 * HD),
        ],
        1,
    )
    d_shared = by_core[:, :, HD : 2 * HD]

    mine = [d_ffn] + [send(d_ffn, "y", k) for k in range(1, 4)]
    mine = jnp.stack(mine)
    other = send(mine, "core", 1)
    both = jnp.where(first, jnp.stack([mine, other], 1), jnp.stack([other, mine], 1))
    twice = jnp.concatenate([both[::-1], both[::-1]], 0)
    ordered = lax.dynamic_slice_in_dim(twice, 3 - y, 4, 0)
    ordered = ordered.reshape(8, shard_rows, 3, ff_pad)[..., :ff_local]
    d_all = ordered.transpose(1, 2, 0, 3).reshape(shard_rows, 3, 8 * ff_local).astype(F32)
    return (
        result[None],
        grad_tokens[None],
        d_gains,
        d_head,
        d_split,
        d_shared,
        d_all[:, :2],
        d_all[:, 2],
    )


def solution(mesh):
    fine = Mesh(mesh.devices.reshape(4, 2, 4, 2, 2), ("z", "xh", "y", "core", "tp"))
    fsdp, ctx, tp = ("z", "xh"), ("y", "core"), "tp"
    in_specs = (
        P(fsdp, ctx, None),
        P(fsdp, ctx),
        P(fsdp, None),
        P(),
        P(fsdp, None, tp),
        P(fsdp, None, None),
        P(fsdp, None, tp),
        P(fsdp, tp),
        P(fsdp, ctx, None),
    )
    out_specs = (
        P(fsdp, ctx, None),
        P(fsdp, ctx, None),
        P(fsdp, None),
        P(),
        P(fsdp, None, tp),
        P(fsdp, None, None),
        P(fsdp, None, tp),
        P(fsdp, tp),
    )
    return jax.shard_map(
        on_device, mesh=fine, in_specs=in_specs, out_specs=out_specs, check_vma=False
    )
```

time: 1130 us -> 432 us (0.38)
  waiting for transfers between devices: 788 us -> 235 us
  blocking collectives: 124 us -> 0 us
  starting transfers between devices: 0.89 us -> 76.5 us
  local copies, waits for them, and re-layouts: 109 us -> 49.3 us
  matrix products: 62.7 us -> 23.2 us
  between operations: 15.2 us -> 2.2 us
    reduce_scatter x3 -> x0, waiting for transfers between devices: 395 us -> none  [the longest x1 283 us: on_device(): lax.psum_scatter(jnp.concatenate([split_part, shared_part], axis=1).astyp...]
    all_gather x4 -> x0, waiting for transfers between devices: 287 us -> none  [the longest x1 174 us: on_device(): lax.all_gather(ffn_gate_up, 'fsdp', axis=0, tiled=True)]
    ppermute x0 -> x67, waiting for transfers between devices: none -> 235 us  [send(): return lax.ppermute(array, axis, [(i, (i + shift) % n) for i in range(n)])]
    psum x5 -> x0, waiting for transfers between devices: 104 us -> none  [the longest x1 32.9 us: on_device(): branch_attn = lax.psum(dot_last(attended_bf, w_output), 'tp')]
    ppermute x0 -> x67, starting transfers between devices: none -> 76.5 us  [send(): return lax.ppermute(array, axis, [(i, (i + shift) % n) for i in range(n)])]
    psum x1 -> x0, blocking collectives: 67 us -> none  [on_device(): d_head = lax.psum(head_terms, ('fsdp', 'ctx', 'tp'))]
    all_gather x3 -> x0, blocking collectives: 56.7 us -> none  [the longest x1 27.6 us: on_device(): lax.all_gather(norm_gains, 'fsdp', axis=0, tiled=True)]
    concatenate x1 -> x2, local copies, waits for them, and re-layouts: 47.7 us -> 0.34 us  [gather_tokens(): return jnp.concatenate([mine, send(mine, 'core', 1)], 0)]
  transfers between devices with their start and end apart: 12 -> 67, of which waited for: 12 -> 43; matrix products, arithmetic and copies ran while one was open for 8% -> 20% of each run, Pallas kernels for 0% -> 0%
where the time goes in v1:
time: 432 us; the launch traced here: 425 us
  waiting for transfers between devices  235 us (54%)
  starting transfers between devices  76.5 us (18%)
  local copies, waits for them, and re-layouts  49.3 us (11%)
  other arithmetic  38.5 us (9%)
  matrix products  23.2 us (5%)
    ppermute x67, waiting for transfers between devices, send(): return lax.ppermute(array, axis, [(i, (i + shift) % n) for i in range(n)])  235 us
    ppermute x67, starting transfers between devices, send(): return lax.ppermute(array, axis, [(i, (i + shift) % n) for i in range(n)])  76.5 us
    convert_element_type x2, local copies, waits for them, and re-layouts, on_device(): ordered.transpose(1, 2, 0, 3).reshape(shard_rows, 3, 8 * ff_local)  15.3 us
    dot_general x6, matrix products, dot(): return jnp.dot(left, right, preferred_element_type=F32)  9.98 us
    unnamed x75, local copies, waits for them, and re-layouts  8.88 us
  transfers between devices with their start and end apart: 67, of which 43 were waited for; matrix products, arithmetic and copies ran while one was open for 20% of the time, Pallas kernels for 0%

profile of v1, /device:TPU:1, one launch (start us, length us, event | category | flops | bytes accessed | tf_op | source)
XLA Modules:
  0.0 424.6 jit_solution(9503214132784677845)
XLA Ops:
  15.9 3.4 collective-permute-start.3
  20.8 5.3 %collective-permute-done.2 = bf16[288,640]{1,0:T(8,128)(2,1)} collective-permute-done((bf16[288,640]{1,0:T(8,128)(2,1)S(1)}, bf16[288,640]{1,0:T(8,128)(2,1)}, u32[]{:S(2)}, u32[]{:S(2)}) %collective-permute-start.2) | collective-permute-done | bytes 368672 | tf_op jit(solution)/shard_map/ppermute | solution.py:56
  27.2 7.7 %collective-permute-done.3 = bf16[288,640]{1,0:T(8,128)(2,1)S(1)} collective-permute-done((bf16[288,640]{1,0:T(8,128)(2,1)S(1)}, bf16[288,640]{1,0:T(8,128)(2,1)S(1)}, u32[]{:S(2)}, u32[]{:S(2)}) %collective-permute-start.3) | collective-permute-done | bytes 368672 | tf_op jit(solution)/shard_map/ppermute | solution.py:56
  47.8 4.1 collective-permute-done.8
  52.6 3.8 collective-permute-done.6
  63.8 43.8 %collective-permute-done.11 = bf16[288,1792]{1,0:T(8,128)(2,1)S(1)} collective-permute-done((bf16[288,1792]{1,0:T(8,128)(2,1)S(1)}, bf16[288,1792]{1,0:T(8,128)(2,1)S(1)}, u32[]{:S(2)}, u32[]{:S(2)}) %collective-permute-start.11) | collective-permute-done | bytes 1032224 | tf_op jit(solution)/shard_map/ppermute | solution.py:56
  111.6 7.0 %collective-permute-done.15 = bf16[128,1152]{1,0:T(8,128)(2,1)S(1)} collective-permute-done((bf16[128,1152]{1,0:T(8,128)(2,1)S(1)}, bf16[128,1152]{1,0:T(8,128)(2,1)S(1)}, u32[]{:S(2)}, u32[]{:S(2)}) %collective-permute-start.15) | collective-permute-done | bytes 294944 | tf_op jit(solution)/shard_map/ppermute | solution.py:56
  121.8 5.9 %collective-permute-done.18 = bf16[128,1152]{1,0:T(8,128)(2,1)S(1)} collective-permute-done((bf16[128,1152]{1,0:T(8,128)(2,1)S(1)}, bf16[128,1152]{1,0:T(8,128)(2,1)S(1)}, u32[]{:S(2)}, u32[]{:S(2)}) %collective-permute-start.18) | collective-permute-done | bytes 294944 | tf_op jit(solution)/shard_map/ppermute | solution.py:56
  129.2 8.1 %collective-permute-done.16 = bf16[128,1152]{1,0:T(8,128)(2,1)S(1)} collective-permute-done((bf16[128,1152]{1,0:T(8,128)(2,1)S(1)}, bf16[128,1152]{1,0:T(8,128)(2,1)S(1)}, u32[]{:S(2)}, u32[]{:S(2)}) %collective-permute-start.16) | collective-permute-done | bytes 294944 | tf_op jit(solution)/shard_map/ppermute | solution.py:56
  151.7 5.9 %collective-permute-done.21 = bf16[128,1152]{1,0:T(8,128)(2,1)S(1)} collective-permute-done((bf16[128,1152]{1,0:T(8,128)(2,1)S(1)}, bf16[128,1152]{1,0:T(8,128)(2,1)S(1)}, u32[]{:S(2)}, u32[]{:S(2)}) %collective-permute-start.21) | collective-permute-done | bytes 294944 | tf_op jit(solution)/shard_map/ppermute | solution.py:56
  157.6 8.2 %collective-permute-done.23 = bf16[128,1152]{1,0:T(8,128)(2,1)S(1)} collective-permute-done((bf16[128,1152]{1,0:T(8,128)(2,1)S(1)}, bf16[128,1152]{1,0:T(8,128)(2,1)S(1)}, u32[]{:S(2)}, u32[]{:S(2)}) %collective-permute-start.23) | collective-permute-done | bytes 294944 | tf_op jit(solution)/shard_map/ppermute | solution.py:56
  167.3 5.8 %collective-permute-done.24 = bf16[128,1152]{1,0:T(8,128)(2,1)S(1)} collective-permute-done((bf16[128,1152]{1,0:T(8,128)(2,1)S(1)}, bf16[128,1152]{1,0:T(8,128)(2,1)S(1)}, u32[]{:S(2)}, u32[]{:S(2)}) %collective-permute-start.24) | collective-permute-done | bytes 294944 | tf_op jit(solution)/shard_map/ppermute | solution.py:56
  176.7 4.2 collective-permute-done.27
  183.2 9.0 %collective-permute-done.25 = bf16[128,1152]{1,0:T(8,128)(2,1)S(1)} collective-permute-done((bf16[128,1152]{1,0:T(8,128)(2,1)S(1)}, bf16[128,1152]{1,0:T(8,128)(2,1)S(1)}, u32[]{:S(2)}, u32[]{:S(2)}) %collective-permute-start.25) | collective-permute-done | bytes 294944 | tf_op jit(solution)/shard_map/ppermute | solution.py:56
  203.5 3.8 convolution_convert_fusion
  219.3 3.9 collective-permute-done.32
  223.2 6.3 %collective-permute-done.31 = bf16[128,1152]{1,0:T(8,128)(2,1)} collective-permute-done((bf16[128,1152]{1,0:T(8,128)(2,1)}, bf16[128,1152]{1,0:T(8,128)(2,1)}, u32[]{:S(2)}, u32[]{:S(2)}) %collective-permute-start.31) | collective-permute-done | bytes 294944 | tf_op jit(solution)/shard_map/ppermute | solution.py:56
  234.9 20.0 %collective-permute-done.61 = bf16[288,1536]{1,0:T(8,128)(2,1)} collective-permute-done((bf16[288,1536]{1,0:T(8,128)(2,1)}, bf16[288,1536]{1,0:T(8,128)(2,1)}, u32[]{:S(2)}, u32[]{:S(2)}) %collective-permute-start.61) | collective-permute-done | bytes 884768 | tf_op jit(solution)/shard_map/ppermute | solution.py:56
  262.0 8.1 %collective-permute-done.62 = bf16[144,1536]{1,0:T(8,128)(2,1)S(1)} collective-permute-done((bf16[144,1536]{1,0:T(8,128)(2,1)S(1)}, bf16[144,1536]{1,0:T(8,128)(2,1)S(1)}, u32[]{:S(2)}, u32[]{:S(2)}) %collective-permute-start.62) | collective-permute-done | bytes 442400 | tf_op jit(solution)/shard_map/ppermute | solution.py:56
  282.4 11.4 %collective-permute-done.63 = bf16[144,1536]{1,0:T(8,128)(2,1)S(1)} collective-permute-done((bf16[144,1536]{1,0:T(8,128)(2,1)S(1)}, bf16[144,1536]{1,0:T(8,128)(2,1)S(1)}, u32[]{:S(2)}, u32[]{:S(2)}) %collective-permute-start.63) | collective-permute-done | bytes 442400 | tf_op jit(solution)/shard_map/ppermute | solution.py:56
  318.6 8.1 %collective-permute-done.51 = bf16[288,768]{1,0:T(8,128)(2,1)S(1)} collective-permute-done((bf16[288,768]{1,0:T(8,128)(2,1)S(1)}, bf16[288,768]{1,0:T(8,128)(2,1)S(1)}, u32[]{:S(2)}, u32[]{:S(2)}) %collective-permute-start.51) | collective-permute-done | bytes 442400 | tf_op jit(solution)/shard_map/ppermute | solution.py:56
  328.4 9.9 %collective-permute-done.53 = bf16[288,768]{1,0:T(8,128)(2,1)S(1)} collective-permute-done((bf16[288,768]{1,0:T(8,128)(2,1)S(1)}, bf16[288,768]{1,0:T(8,128)(2,1)S(1)}, u32[]{:S(2)}, u32[]{:S(2)}) %collective-permute-start.53) | collective-permute-done | bytes 442400 | tf_op jit(solution)/shard_map/ppermute | solution.py:56
  342.6 6.2 %collective-permute-done.43 = f32[5,1152]{1,0:T(8,128)S(1)} collective-permute-done((f32[5,1152]{1,0:T(8,128)S(1)}, f32[5,1152]{1,0:T(8,128)S(1)}, u32[]{:S(2)}, u32[]{:S(2)}) %collective-permute-start.43) | collective-permute-done | bytes 23072 | tf_op jit(solution)/shard_map/ppermute | solution.py:56
  362.3 3.8 maximum_select_fusion
  368.2 3.3 fusion
  371.5 6.0 %reshape.412 = bf16[8,144,3,512]{3,2,1,0:T(4,128)(2,1)} reshape(bf16[4,2,144,1536]{3,2,1,0:T(8,128)(2,1)S(1)} %fusion) | data formatting | bytes 7077888 | tf_op jit(solution)/shard_map/reshape | solution.py:339
  377.5 3.7 convert_bitcast_fusion
  381.2 6.9 %copy.41 = f32[144,3,8,432]{3,2,0,1:T(8,128)} copy(f32[144,3,8,432]{3,1,0,2:T(4,128)S(1)} %convert_bitcast_fusion) | data formatting | bytes 11943936 | tf_op jit(solution)/shard_map/convert_element_type | solution.py:340
  388.1 8.4 %reshape.417 = f32[144,3,3456]{2,0,1:T(8,128)} reshape(f32[144,3,8,432]{3,2,0,1:T(8,128)} %copy.41) | data formatting | bytes 11943936 | tf_op jit(solution)/shard_map/convert_element_type | solution.py:340
  401.6 4.0 copy.44
  407.7 4.3 %collective-permute-done.55 = bf16[144,768]{1,0:T(8,128)(2,1)S(1)} collective-permute-done((bf16[144,768]{1,0:T(8,128)(2,1)}, bf16[144,768]{1,0:T(8,128)(2,1)S(1)}, u32[]{:S(2)}, u32[]{:S(2)}) %collective-permute-start.55) | collective-permute-done | bytes 221216 | tf_op jit(solution)/shard_map/ppermute | solution.py:56
  413.3 6.2 %collective-permute-start.58 = (bf16[144,768]{1,0:T(8,128)(2,1)S(1)}, bf16[144,768]{1,0:T(8,128)(2,1)S(1)}, u32[]{:S(2)}, u32[]{:S(2)}) collective-permute-start(bf16[144,768]{1,0:T(8,128)(2,1)S(1)} %add_convert_fusion), channel_id=1, source_target_pairs={{0,2},{2,0},{1,3},{3,1},{4,6},{6,4},{5,7},{7,5},{8,10},{10,8},{9,1... | collective-permute-start | bytes 663560 | tf_op jit(solution)/shard_map/ppermute | solution.py:56
  (336 shorter events, 175.9 us)
Async XLA Ops:
  1.4 37.9 %collective-permute-start = (f32[1,128]{1,0:T(1,128)S(1)}, f32[1,128]{1,0:T(1,128)S(1)}, u32[]{:S(2)}, u32[]{:S(2)}) collective-permute-start(f32[1,128]{1,0:T(1,128)S(1)} %convert_element_type.257), channel_id=1, source_target_pairs={{0,2},{2,0},{1,3},{3,1},{4,6},{6,4},{5,7},{7,5},{8,10},{10,8},{9,1... | collective-permute-start | bytes 1544 | tf_op jit(solution)/shard_map/ppermute | solution.py:56
  12.4 44.6 %collective-permute-start.10 = (bf16[144,1792]{1,0:T(8,128)(2,1)}, bf16[144,1792]{1,0:T(8,128)(2,1)S(1)}, u32[]{:S(2)}, u32[]{:S(2)}) collective-permute-start(bf16[144,1792]{1,0:T(8,128)(2,1)} %get-tuple-element.101), channel_id=1, source_target_pairs={{0,16},{16,0},{1,17},{17,1},{2,18},{18,2},{3,19},{19,3},{4,20},{20... | collective-permute-start | bytes 1548296 | tf_op jit(solution)/shard_map/ppermute | solution.py:56
  14.0 12.2 %collective-permute-start.2 = (bf16[288,640]{1,0:T(8,128)(2,1)S(1)}, bf16[288,640]{1,0:T(8,128)(2,1)}, u32[]{:S(2)}, u32[]{:S(2)}) collective-permute-start(bf16[288,640]{1,0:T(8,128)(2,1)S(1)} %maximum_select_fusion.5), channel_id=1, source_target_pairs={{0,32},{32,64},{64,96},{96,0},{1,33},{33,65},{65,97},{97,1},{2,34}... | collective-permute-start | bytes 1105928 | tf_op jit(solution)/shard_map/ppermute | solution.py:56
  15.9 18.9 %collective-permute-start.3 = (bf16[288,640]{1,0:T(8,128)(2,1)S(1)}, bf16[288,640]{1,0:T(8,128)(2,1)S(1)}, u32[]{:S(2)}, u32[]{:S(2)}) collective-permute-start(bf16[288,640]{1,0:T(8,128)(2,1)S(1)} %maximum_select_fusion.5), channel_id=1, source_target_pairs={{0,64},{32,96},{64,0},{96,32},{1,65},{33,97},{65,1},{97,33},{2,66}... | collective-permute-start | bytes 1105928 | tf_op jit(solution)/shard_map/ppermute | solution.py:56
  19.8 15.1 %collective-permute-start.4 = (bf16[288,640]{1,0:T(8,128)(2,1)S(1)}, bf16[288,640]{1,0:T(8,128)(2,1)S(1)}, u32[]{:S(2)}, u32[]{:S(2)}) collective-permute-start(bf16[288,640]{1,0:T(8,128)(2,1)S(1)} %maximum_select_fusion.5), channel_id=1, source_target_pairs={{0,96},{32,0},{64,32},{96,64},{1,97},{33,1},{65,33},{97,65},{2,98}... | collective-permute-start | bytes 1105928 | tf_op jit(solution)/shard_map/ppermute | solution.py:56
  57.3 50.6 %collective-permute-start.13 = (bf16[288,1792]{1,0:T(8,128)(2,1)S(1)}, bf16[288,1792]{1,0:T(8,128)(2,1)S(1)}, u32[]{:S(2)}, u32[]{:S(2)}) collective-permute-start(bf16[288,1792]{1,0:T(8,128)(2,1)S(1)} %maximum_select_fusion.2), channel_id=1, source_target_pairs={{0,96},{32,0},{64,32},{96,64},{1,97},{33,1},{65,33},{97,65},{2,98}... | collective-permute-start | bytes 3096584 | tf_op jit(solution)/shard_map/ppermute | solution.py:56
  59.3 48.5 %collective-permute-start.12 = (bf16[288,1792]{1,0:T(8,128)(2,1)S(1)}, bf16[288,1792]{1,0:T(8,128)(2,1)S(1)}, u32[]{:S(2)}, u32[]{:S(2)}) collective-permute-start(bf16[288,1792]{1,0:T(8,128)(2,1)S(1)} %maximum_select_fusion.2), channel_id=1, source_target_pairs={{0,64},{32,96},{64,0},{96,32},{1,65},{33,97},{65,1},{97,33},{2,66}... | collective-permute-start | bytes 3096584 | tf_op jit(solution)/shard_map/ppermute | solution.py:56
  60.6 47.1 %collective-permute-start.11 = (bf16[288,1792]{1,0:T(8,128)(2,1)S(1)}, bf16[288,1792]{1,0:T(8,128)(2,1)S(1)}, u32[]{:S(2)}, u32[]{:S(2)}) collective-permute-start(bf16[288,1792]{1,0:T(8,128)(2,1)S(1)} %maximum_select_fusion.2), channel_id=1, source_target_pairs={{0,32},{32,64},{64,96},{96,0},{1,33},{33,65},{65,97},{97,1},{2,34}... | collective-permute-start | bytes 3096584 | tf_op jit(solution)/shard_map/ppermute | solution.py:56
  121.0 16.4 %collective-permute-start.16 = (bf16[128,1152]{1,0:T(8,128)(2,1)S(1)}, bf16[128,1152]{1,0:T(8,128)(2,1)S(1)}, u32[]{:S(2)}, u32[]{:S(2)}) collective-permute-start(bf16[128,1152]{1,0:T(8,128)(2,1)S(1)} %get-tuple-element.64), channel_id=1, source_target_pairs={{0,4},{4,8},{8,12},{12,0},{1,5},{5,9},{9,13},{13,1},{2,6},{6,10},{... | collective-permute-start | bytes 884744 | tf_op jit(solution)/shard_map/ppermute | solution.py:56
  150.0 15.8 %collective-permute-start.23 = (bf16[128,1152]{1,0:T(8,128)(2,1)S(1)}, bf16[128,1152]{1,0:T(8,128)(2,1)S(1)}, u32[]{:S(2)}, u32[]{:S(2)}) collective-permute-start(bf16[128,1152]{1,0:T(8,128)(2,1)S(1)} %get-tuple-element.83), channel_id=1, source_target_pairs={{0,4},{4,8},{8,12},{12,0},{1,5},{5,9},{9,13},{13,1},{2,6},{6,10},{... | collective-permute-start | bytes 884744 | tf_op jit(solution)/shard_map/ppermute | solution.py:56
  151.3 14.6 %collective-permute-start.22 = (bf16[128,1152]{1,0:T(8,128)(2,1)S(1)}, bf16[128,1152]{1,0:T(8,128)(2,1)S(1)}, u32[]{:S(2)}, u32[]{:S(2)}) collective-permute-start(bf16[128,1152]{1,0:T(8,128)(2,1)S(1)} %get-tuple-element.84), channel_id=1, source_target_pairs={{0,8},{4,12},{8,0},{12,4},{1,9},{5,13},{9,1},{13,5},{2,10},{6,14},... | collective-permute-start | bytes 884744 | tf_op jit(solution)/shard_map/ppermute | solution.py:56
  175.9 16.3 %collective-permute-start.25 = (bf16[128,1152]{1,0:T(8,128)(2,1)S(1)}, bf16[128,1152]{1,0:T(8,128)(2,1)S(1)}, u32[]{:S(2)}, u32[]{:S(2)}) collective-permute-start(bf16[128,1152]{1,0:T(8,128)(2,1)S(1)} %get-tuple-element.60), channel_id=1, source_target_pairs={{0,4},{4,8},{8,12},{12,0},{1,5},{5,9},{9,13},{13,1},{2,6},{6,10},{... | collective-permute-start | bytes 884744 | tf_op jit(solution)/shard_map/ppermute | solution.py:56
  212.2 21.1 %collective-permute-start.59 = (bf16[288,1536]{1,0:T(8,128)(2,1)}, bf16[288,1536]{1,0:T(8,128)(2,1)}, u32[]{:S(2)}, u32[]{:S(2)}) collective-permute-start(bf16[288,1536]{1,0:T(8,128)(2,1)} %get-tuple-element.69), channel_id=1, source_target_pairs={{0,96},{32,0},{64,32},{96,64},{1,97},{33,1},{65,33},{97,65},{2,98}... | collective-permute-start | bytes 2654216 | tf_op jit(solution)/shard_map/ppermute | solution.py:56
  212.5 22.4 %collective-permute-start.60 = (bf16[288,1536]{1,0:T(8,128)(2,1)}, bf16[288,1536]{1,0:T(8,128)(2,1)}, u32[]{:S(2)}, u32[]{:S(2)}) collective-permute-start(bf16[288,1536]{1,0:T(8,128)(2,1)} %get-tuple-element.70), channel_id=1, source_target_pairs={{0,64},{32,96},{64,0},{96,32},{1,65},{33,97},{65,1},{97,33},{2,66}... | collective-permute-start | bytes 2654216 | tf_op jit(solution)/shard_map/ppermute | solution.py:56
  213.8 41.1 %collective-permute-start.61 = (bf16[288,1536]{1,0:T(8,128)(2,1)}, bf16[288,1536]{1,0:T(8,128)(2,1)}, u32[]{:S(2)}, u32[]{:S(2)}) collective-permute-start(bf16[288,1536]{1,0:T(8,128)(2,1)} %get-tuple-element.71), channel_id=1, source_target_pairs={{0,32},{32,64},{64,96},{96,0},{1,33},{33,65},{65,97},{97,1},{2,34}... | collective-permute-start | bytes 2654216 | tf_op jit(solution)/shard_map/ppermute | solution.py:56
  230.9 29.2 %collective-permute-start.33 = (bf16[128,1152]{1,0:T(8,128)(2,1)S(1)}, bf16[128,1152]{1,0:T(8,128)(2,1)S(1)}, u32[]{:S(2)}, u32[]{:S(2)}) collective-permute-start(bf16[128,1152]{1,0:T(8,128)(2,1)S(1)} %fusion.44), channel_id=1, source_target_pairs={{0,1},{1,0},{2,3},{3,2},{4,5},{5,4},{6,7},{7,6},{8,9},{9,8},{10,11... | collective-permute-start | bytes 884744 | tf_op jit(solution)/shard_map/ppermute | solution.py:56
  257.2 12.8 %collective-permute-start.62 = (bf16[144,1536]{1,0:T(8,128)(2,1)S(1)}, bf16[144,1536]{1,0:T(8,128)(2,1)S(1)}, u32[]{:S(2)}, u32[]{:S(2)}) collective-permute-start(bf16[144,1536]{1,0:T(8,128)(2,1)S(1)} %dynamic-slice_bitcast_fusion), channel_id=1, source_target_pairs={{0,16},{16,0},{1,17},{17,1},{2,18},{18,2},{3,19},{19,3},{4,20},{20... | collective-permute-start | bytes 1327112 | tf_op jit(solution)/shard_map/ppermute | solution.py:56
  261.1 12.0 %collective-permute-start.34 = (bf16[128,1152]{1,0:T(8,128)(2,1)S(1)}, bf16[128,1152]{1,0:T(8,128)(2,1)S(1)}, u32[]{:S(2)}, u32[]{:S(2)}) collective-permute-start(bf16[128,1152]{1,0:T(8,128)(2,1)S(1)} %subtract_convert_fusion), channel_id=1, source_target_pairs={{0,2},{2,0},{1,3},{3,1},{4,6},{6,4},{5,7},{7,5},{8,10},{10,8},{9,1... | collective-permute-start | bytes 884744 | tf_op jit(solution)/shard_map/ppermute | solution.py:56
  270.8 11.6 %collective-permute-start.64 = (bf16[144,1536]{1,0:T(8,128)(2,1)S(1)}, bf16[144,1536]{1,0:T(8,128)(2,1)S(1)}, u32[]{:S(2)}, u32[]{:S(2)}) collective-permute-start(bf16[144,1536]{1,0:T(8,128)(2,1)S(1)} %fusion.37), channel_id=1, source_target_pairs={{0,8},{4,12},{8,0},{12,4},{1,9},{5,13},{9,1},{13,5},{2,10},{6,14},... | collective-permute-start | bytes 1327112 | tf_op jit(solution)/shard_map/ppermute | solution.py:56
  273.2 20.7 %collective-permute-start.63 = (bf16[144,1536]{1,0:T(8,128)(2,1)S(1)}, bf16[144,1536]{1,0:T(8,128)(2,1)S(1)}, u32[]{:S(2)}, u32[]{:S(2)}) collective-permute-start(bf16[144,1536]{1,0:T(8,128)(2,1)S(1)} %fusion.37), channel_id=1, source_target_pairs={{0,4},{4,8},{8,12},{12,0},{1,5},{5,9},{9,13},{13,1},{2,6},{6,10},{... | collective-permute-start | bytes 1327112 | tf_op jit(solution)/shard_map/ppermute | solution.py:56
  276.0 20.4 %collective-permute-start.35 = (bf16[1024,256]{1,0:T(8,128)(2,1)S(1)}, bf16[1024,256]{1,0:T(8,128)(2,1)S(1)}, u32[]{:S(2)}, u32[]{:S(2)}) collective-permute-start(bf16[1024,256]{1,0:T(8,128)(2,1)S(1)} %bitcast.189), channel_id=1, source_target_pairs={{0,2},{2,0},{1,3},{3,1},{4,6},{6,4},{5,7},{7,5},{8,10},{10,8},{9,1... | collective-permute-start | bytes 1572872 | tf_op jit(solution)/shard_map/ppermute | solution.py:56
  295.9 65.1 %collective-permute-start.66 = (bf16[4,144,1536]{2,1,0:T(8,128)(2,1)}, bf16[4,144,1536]{2,1,0:T(8,128)(2,1)}, u32[]{:S(2)}, u32[]{:S(2)}) collective-permute-start(bf16[4,144,1536]{2,1,0:T(8,128)(2,1)} %get-tuple-element.75), channel_id=1, source_target_pairs={{0,2},{2,0},{1,3},{3,1},{4,6},{6,4},{5,7},{7,5},{8,10},{10,8},{9,1... | collective-permute-start | bytes 5308424 | tf_op jit(solution)/shard_map/ppermute | solution.py:56
  315.0 11.8 %collective-permute-start.51 = (bf16[288,768]{1,0:T(8,128)(2,1)S(1)}, bf16[288,768]{1,0:T(8,128)(2,1)S(1)}, u32[]{:S(2)}, u32[]{:S(2)}) collective-permute-start(bf16[288,768]{1,0:T(8,128)(2,1)S(1)} %get-tuple-element.76), channel_id=1, source_target_pairs={{0,96},{32,0},{64,32},{96,64},{1,97},{33,1},{65,33},{97,65},{2,98}... | collective-permute-start | bytes 1327112 | tf_op jit(solution)/shard_map/ppermute | solution.py:56
  315.1 13.3 %collective-permute-start.52 = (bf16[288,768]{1,0:T(8,128)(2,1)S(1)}, bf16[288,768]{1,0:T(8,128)(2,1)S(1)}, u32[]{:S(2)}, u32[]{:S(2)}) collective-permute-start(bf16[288,768]{1,0:T(8,128)(2,1)S(1)} %get-tuple-element.77), channel_id=1, source_target_pairs={{0,64},{32,96},{64,0},{96,32},{1,65},{33,97},{65,1},{97,33},{2,66}... | collective-permute-start | bytes 1327112 | tf_op jit(solution)/shard_map/ppermute | solution.py:56
  316.5 21.8 %collective-permute-start.53 = (bf16[288,768]{1,0:T(8,128)(2,1)S(1)}, bf16[288,768]{1,0:T(8,128)(2,1)S(1)}, u32[]{:S(2)}, u32[]{:S(2)}) collective-permute-start(bf16[288,768]{1,0:T(8,128)(2,1)S(1)} %get-tuple-element.78), channel_id=1, source_target_pairs={{0,32},{32,64},{64,96},{96,0},{1,33},{33,65},{65,97},{97,1},{2,34}... | collective-permute-start | bytes 1327112 | tf_op jit(solution)/shard_map/ppermute | solution.py:56
  317.3 21.2 %collective-permute-start.41 = (bf16[128,1152]{1,0:T(8,128)(2,1)S(1)}, bf16[128,1152]{1,0:T(8,128)(2,1)S(1)}, u32[]{:S(2)}, u32[]{:S(2)}) collective-permute-start(bf16[128,1152]{1,0:T(8,128)(2,1)S(1)} %fusion.41), channel_id=1, source_target_pairs={{0,1},{1,0},{2,3},{3,2},{4,5},{5,4},{6,7},{7,6},{8,9},{9,8},{10,11... | collective-permute-start | bytes 884744 | tf_op jit(solution)/shard_map/ppermute | solution.py:56
  339.4 16.6 %collective-permute-start.54 = (bf16[144,768]{1,0:T(8,128)(2,1)S(1)}, bf16[144,768]{1,0:T(8,128)(2,1)S(1)}, u32[]{:S(2)}, u32[]{:S(2)}) collective-permute-start(bf16[144,768]{1,0:T(8,128)(2,1)S(1)} %dynamic-slice_bitcast_fusion.1), channel_id=1, source_target_pairs={{0,16},{16,0},{1,17},{17,1},{2,18},{18,2},{3,19},{19,3},{4,20},{20... | collective-permute-start | bytes 663560 | tf_op jit(solution)/shard_map/ppermute | solution.py:56
  356.7 51.1 %collective-permute-start.57 = (bf16[144,768]{1,0:T(8,128)(2,1)}, bf16[144,768]{1,0:T(8,128)(2,1)}, u32[]{:S(2)}, u32[]{:S(2)}) collective-permute-start(bf16[144,768]{1,0:T(8,128)(2,1)} %fusion.70), channel_id=1, source_target_pairs={{0,12},{4,0},{8,4},{12,8},{1,13},{5,1},{9,5},{13,9},{2,14},{6,2},{... | collective-permute-start | bytes 663560 | tf_op jit(solution)/shard_map/ppermute | solution.py:56
  357.7 50.0 %collective-permute-start.56 = (bf16[144,768]{1,0:T(8,128)(2,1)}, bf16[144,768]{1,0:T(8,128)(2,1)}, u32[]{:S(2)}, u32[]{:S(2)}) collective-permute-start(bf16[144,768]{1,0:T(8,128)(2,1)} %fusion.70), channel_id=1, source_target_pairs={{0,4},{4,8},{8,12},{12,0},{1,5},{5,9},{9,13},{13,1},{2,6},{6,10},{... | collective-permute-start | bytes 663560 | tf_op jit(solution)/shard_map/ppermute | solution.py:56
  359.5 46.1 %collective-permute-start.50 = (f32[5,1152]{1,0:T(8,128)}, f32[5,1152]{1,0:T(8,128)}, u32[]{:S(2)}, u32[]{:S(2)}) collective-permute-start(f32[5,1152]{1,0:T(8,128)} %add_add_fusion.1), channel_id=1, source_target_pairs={{0,96},{32,0},{64,32},{96,64},{1,97},{33,1},{65,33},{97,65},{2,98}... | collective-permute-start | bytes 69128 | tf_op jit(solution)/shard_map/ppermute | solution.py:56
  360.3 46.6 %collective-permute-start.49 = (f32[5,1152]{1,0:T(8,128)}, f32[5,1152]{1,0:T(8,128)}, u32[]{:S(2)}, u32[]{:S(2)}) collective-permute-start(f32[5,1152]{1,0:T(8,128)} %add_add_fusion.1), channel_id=1, source_target_pairs={{0,32},{32,64},{64,96},{96,0},{1,33},{33,65},{65,97},{97,1},{2,34}... | collective-permute-start | bytes 69128 | tf_op jit(solution)/shard_map/ppermute | solution.py:56
  361.0 45.9 %collective-permute-start.48 = (f32[5,1152]{1,0:T(8,128)}, f32[5,1152]{1,0:T(8,128)}, u32[]{:S(2)}, u32[]{:S(2)}) collective-permute-start(f32[5,1152]{1,0:T(8,128)} %add_add_fusion.1), channel_id=1, source_target_pairs={{0,64},{32,96},{64,0},{96,32},{1,65},{33,97},{65,1},{97,33},{2,66}... | collective-permute-start | bytes 69128 | tf_op jit(solution)/shard_map/ppermute | solution.py:56
  (67 other events, 625.3 us)
